TPU v7x, 32 devices: a whole 2x2x4 slice. The times are simulated.
32 devices in a mesh: tm: 2 (over y), pts: 16 (over z, x, core).
Axes of the slice: x: 2, y: 2, z: 4, core: 2. Of those that a mesh axis runs over, the one named last changes fastest.
Arguments:
- precip: float32 [512, 16384], P('tm', 'pts'), may hold values from -150 to 300, as said below
- thresholds: float32 [64], replicated, may hold values from -1 to 5
- bin_index: int32 [16384], P('pts'), may hold values from 0 to 63
- test_matrix: float32 [512, 256], P('tm'), may hold values from -0.25 to 0.25
Outputs:
- basis: float32 [16384, 256], P(('pts', 'tm'))
- factor: float32 [256, 256], replicated
Inputs may be any that keep to these rules, and one draw needn't show every extreme that they name: `precip`: precipitation records.
All inputs are finite; a program needn't handle non-finite values.
Results may differ from a plain program's by a relative error of at most 0.0003.
Values sent between devices are 32-bit elements; how exact they have to be, the bound alone decides.
No kernel may reach another device: no remote copies, remote signals or barrier semaphores. Data moves between devices by JAX's collectives and lax.ppermute only.
A program may use at most 64 MiB of HBM per device.

v0:
```python
import math
import jax
import jax.numpy as jnp
from jax import lax
from jax.sharding import PartitionSpec as P

HARM = 8
year_days = 365.25


def harmonic_table(day_number):
    phase_base = day_number.astype(jnp.float32)
    columns = [jnp.ones_like(phase_base)]
    for order in range(1, HARM + 1):
        phase = 2.0 * math.pi * order / year_days * phase_base
        columns.append(jnp.cos(phase))
        columns.append(jnp.sin(phase))
    return jnp.stack(columns, 0)


def normal_solve(factor_low, values):
    forward = lax.linalg.triangular_solve(factor_low, values, left_side=True, lower=True)
    return lax.linalg.triangular_solve(
        factor_low, forward, left_side=True, lower=True, transpose_a=True
    )


AXES = ("tm", "pts")


def swap(value, bit):
    total = lax.axis_size("tm") * lax.axis_size("pts")
    return lax.ppermute(value, AXES, [(i, i ^ bit) for i in range(total)])


def all_days(block, count, place, stride):
    pieces = [block] + [swap(block, step * stride) for step in range(1, count)]
    stack = jnp.stack(pieces)
    order = place ^ jnp.arange(count)
    return stack[order].reshape((-1,) + block.shape[1:])


def sum_all(value):
    total = lax.axis_size("tm") * lax.axis_size("pts")
    low = lax.axis_index("pts") % 2
    half = value.shape[0] // 2
    kept = lax.dynamic_slice_in_dim(value, low * half, half, 0)
    sent = lax.dynamic_slice_in_dim(value, (1 - low) * half, half, 0)
    part = kept + swap(sent, 1)
    bit = 2
    while bit < total:
        part = part + swap(part, bit)
        bit *= 2
    other = swap(part, 1)
    return jnp.where(low == 0, jnp.concatenate([part, other], 0), jnp.concatenate([other, part], 0))


def on_device(precip, thresholds, bin_index, test_matrix):
    highest = lax.Precision.HIGHEST
    tm_count = lax.axis_size("tm")
    tm_place = lax.axis_index("tm")
    days_local, points_local = precip.shape
    own_rows = points_local // tm_count
    days_total = days_local * tm_count
    points_total = points_local * lax.axis_size("pts")
    full_table = harmonic_table(jnp.arange(days_total, dtype=jnp.int32))
    normal = jnp.dot(full_table, full_table.T, precision=highest)
    normal_low = jnp.linalg.cholesky(normal)
    one_hot = (
        bin_index[:, None] == jnp.arange(thresholds.shape[0], dtype=jnp.int32)[None, :]
    ).astype(jnp.float32)
    level_local = jnp.dot(one_hot, thresholds, precision=highest)
    series = lax.all_to_all(precip, "tm", split_axis=1, concat_axis=0, tiled=True)
    projections = jnp.dot(full_table, series, precision=highest)
    coefficients = normal_solve(normal_low, projections)
    anomaly = series - lax.dot_general(
        full_table, coefficients, (((0,), (0,)), ((), ())), precision=highest
    )
    level_own = lax.dynamic_slice_in_dim(level_local, tm_place * own_rows, own_rows, 0)
    excess = jnp.maximum(anomaly - level_own[None, :], 0.0)
    sketch = lax.dot_general(
        excess,
        all_days(test_matrix, tm_count, tm_place, lax.axis_size("pts")),
        (((0,), (0,)), ((), ())),
        precision=highest,
    )
    local_cross = jnp.dot(sketch.T, sketch, precision=highest)
    cross = sum_all(local_cross) / points_total
    lower = jnp.linalg.cholesky(cross)
    basis = lax.linalg.triangular_solve(
        lower, sketch, left_side=False, lower=True, transpose_a=True
    )
    return (basis, lower.T)


def solution(mesh):
    in_specs = (P("tm", "pts"), P(), P("pts"), P("tm", None))
    out_specs = (P(("pts", "tm"), None), P())
    return jax.shard_map(
        on_device, mesh=mesh, in_specs=in_specs, out_specs=out_specs, check_vma=False
    )
```

profile of v0, /device:TPU:0, one launch (start us, length us, event | category | flops | bytes accessed | tf_op | source)
XLA Modules:
  0.0 123.8 jit_solution(3260924505696430201)
XLA Ops:
  0.6 0.0 copy-start
  0.6 2.5 %copy.18 = f32[256,1024]{0,1:T(8,128)} copy(f32[256,1024]{1,0:T(8,128)} %param.4) | data formatting | bytes 2097152 | tf_op args[0]
  3.2 4.4 %all-to-all-start = ((f32[256,2,512]{0,2,1:T(8,128)}), f32[256,2,512]{0,2,1:T(8,128)S(1)}, u32[]{:S(2)}, u32[]{:S(2)}) async-start(f32[256,2,512]{0,2,1:T(8,128)} %bitcast), calls=%async_computation | async-start | bytes 2097152 | tf_op jit(solution)/shard_map/all_to_all | solution.py:73
  7.6 2.4 %collective-permute-start = (f32[256,256]{1,0:T(8,128)S(1)}, f32[256,256]{1,0:T(8,128)S(1)}, u32[]{:S(2)}, u32[]{:S(2)}) collective-permute-start(f32[256,256]{1,0:T(8,128)S(1)} %copy-done.1), channel_id=1, source_target_pairs={{0,16},{1,17},{2,18},{3,19},{4,20},{5,21},{6,22},{7,23},{8,24},{9,... | collective-permute-start | bytes 786440 | tf_op jit(solution)/shard_map/ppermute | solution.py:33
  10.0 0.1 fusion.21
  10.0 0.1 fusion.23
  10.1 0.1 fusion.25
  10.2 0.1 fusion.27
  10.3 0.1 fusion.29
  10.4 0.1 fusion.31
  10.5 0.1 fusion.33
  10.5 0.1 fusion.35
  10.6 0.1 stack.8
  10.7 0.2 fusion.40
  10.9 0.1 copy.20
  11.0 1.5 %cholesky.60 = f32[17,17]{1,0:T(8,128)S(1)} custom-call(f32[17,17]{1,0:T(8,128)S(1)} %fusion.20), custom_call_target="Cholesky" | custom-call | tf_op jit(solution)/shard_map/jit(cholesky)/cholesky | solution.py:68
  12.6 0.6 compare_reduce_fusion.2
  13.2 0.7 fusion.15
  13.9 0.0 copy-done.2
  13.9 0.4 fusion.2
  14.4 1.3 %custom-call.22 = f32[1,17,17]{1,2,0:T(8,128)S(1)} custom-call(f32[1,17,17]{2,1,0:T(8,128)S(1)} %fusion.15), custom_call_target="InvertDiagBlocksLowerTriangular" | custom-call | tf_op jit(solution)/shard_map/triangular_solve | solution.py:23
  15.7 0.1 dynamic_slice.9
  15.8 11.8 %collective-permute-done = f32[256,256]{1,0:T(8,128)S(1)} collective-permute-done((f32[256,256]{1,0:T(8,128)S(1)}, f32[256,256]{1,0:T(8,128)S(1)}, u32[]{:S(2)}, u32[]{:S(2)}) %collective-permute-start) | collective-permute-done | bytes 262176 | tf_op jit(solution)/shard_map/ppermute | solution.py:33
  27.7 0.6 gather_fusion
  28.3 0.0 all-to-all-done
  28.3 0.3 copy.19
  28.6 0.6 fusion.41
  29.2 0.2 fusion.18
  29.5 0.2 fusion.16
  29.7 1.1 fusion.1
  30.8 1.8 %fusion.42 = f32[512,256]{1,0:T(8,128)S(1)} fusion(f32[512,512]{1,0:T(8,128)S(1)} %fusion.1, f32[512,256]{1,0:T(8,128)S(1)} %bitcast.71), kind=kOutput, calls=%fused_computation.85 | convolution fusion | flops 805306368 | bytes 2097152 | tf_op jit(solution)/shard_map/dot_general | solution.py:81
  32.6 1.0 fusion.43
  33.7 0.1 collective-permute-start.1
  33.8 1.3 %collective-permute-done.1 = f32[128,256]{0,1:T(8,128)S(1)} collective-permute-done((f32[128,256]{0,1:T(8,128)S(1)}, f32[128,256]{0,1:T(8,128)S(1)}, u32[]{:S(2)}, u32[]{:S(2)}) %collective-permute-start.1) | collective-permute-done | bytes 131104 | tf_op jit(solution)/shard_map/ppermute | solution.py:33
  35.1 1.8 %collective-permute-start.2 = (f32[128,256]{0,1:T(8,128)S(1)}, f32[128,256]{0,1:T(8,128)S(1)}, u32[]{:S(2)}, u32[]{:S(2)}) collective-permute-start(f32[128,256]{0,1:T(8,128)S(1)} %dynamic-slice_add_fusion), channel_id=1, source_target_pairs={{0,2},{1,3},{2,0},{3,1},{4,6},{5,7},{6,4},{7,5},{8,10},{9,11},{10,... | collective-permute-start | bytes 393224 | tf_op jit(solution)/shard_map/ppermute | solution.py:33
  36.9 3.8 %collective-permute-done.2 = f32[128,256]{0,1:T(8,128)S(1)} collective-permute-done((f32[128,256]{0,1:T(8,128)S(1)}, f32[128,256]{0,1:T(8,128)S(1)}, u32[]{:S(2)}, u32[]{:S(2)}) %collective-permute-start.2) | collective-permute-done | bytes 131104 | tf_op jit(solution)/shard_map/ppermute | solution.py:33
  40.7 1.9 %collective-permute-start.3 = (f32[128,256]{0,1:T(8,128)S(1)}, f32[128,256]{0,1:T(8,128)S(1)}, u32[]{:S(2)}, u32[]{:S(2)}) collective-permute-start(f32[128,256]{0,1:T(8,128)S(1)} %add.80), channel_id=1, source_target_pairs={{0,4},{1,5},{2,6},{3,7},{4,0},{5,1},{6,2},{7,3},{8,12},{9,13},{10,... | collective-permute-start | bytes 393224 | tf_op jit(solution)/shard_map/ppermute | solution.py:33
  42.6 3.2 %collective-permute-done.3 = f32[128,256]{0,1:T(8,128)S(1)} collective-permute-done((f32[128,256]{0,1:T(8,128)S(1)}, f32[128,256]{0,1:T(8,128)S(1)}, u32[]{:S(2)}, u32[]{:S(2)}) %collective-permute-start.3) | collective-permute-done | bytes 131104 | tf_op jit(solution)/shard_map/ppermute | solution.py:33
  45.8 2.9 %collective-permute-start.4 = (f32[128,256]{0,1:T(8,128)S(1)}, f32[128,256]{0,1:T(8,128)S(1)}, u32[]{:S(2)}, u32[]{:S(2)}) collective-permute-start(f32[128,256]{0,1:T(8,128)S(1)} %add.81), channel_id=1, source_target_pairs={{0,8},{1,9},{2,10},{3,11},{4,12},{5,13},{6,14},{7,15},{8,0},{9,1},... | collective-permute-start | bytes 393224 | tf_op jit(solution)/shard_map/ppermute | solution.py:33
  48.7 4.6 %collective-permute-done.4 = f32[128,256]{0,1:T(8,128)S(1)} collective-permute-done((f32[128,256]{0,1:T(8,128)S(1)}, f32[128,256]{0,1:T(8,128)S(1)}, u32[]{:S(2)}, u32[]{:S(2)}) %collective-permute-start.4) | collective-permute-done | bytes 131104 | tf_op jit(solution)/shard_map/ppermute | solution.py:33
  53.3 0.7 collective-permute-start.5
  54.0 4.3 %collective-permute-done.5 = f32[128,256]{0,1:T(8,128)S(1)} collective-permute-done((f32[128,256]{0,1:T(8,128)S(1)}, f32[128,256]{0,1:T(8,128)S(1)}, u32[]{:S(2)}, u32[]{:S(2)}) %collective-permute-start.5) | collective-permute-done | bytes 131104 | tf_op jit(solution)/shard_map/ppermute | solution.py:33
  58.3 0.1 collective-permute-start.6
  58.4 1.3 %collective-permute-done.6 = f32[128,256]{0,1:T(8,128)S(1)} collective-permute-done((f32[128,256]{0,1:T(8,128)S(1)}, f32[128,256]{0,1:T(8,128)S(1)}, u32[]{:S(2)}, u32[]{:S(2)}) %collective-permute-start.6) | collective-permute-done | bytes 131104 | tf_op jit(solution)/shard_map/ppermute | solution.py:33
  59.8 0.1 copy.23
  60.0 11.7 %cholesky.123 = f32[128,128]{1,0:T(8,128)S(1)} custom-call(f32[128,128]{1,0:T(8,128)S(1)} %cholesky.153), custom_call_target="Cholesky" | custom-call | tf_op jit(solution)/shard_map/jit(cholesky)/cholesky | solution.py:89
  71.8 10.0 %custom-call.23 = f32[1,128,128]{1,2,0:T(8,128)S(1)} custom-call(f32[1,128,128]{2,1,0:T(8,128)S(1)} %get-tuple-element.31), custom_call_target="InvertDiagBlocksLowerTriangular" | custom-call | tf_op jit(solution)/shard_map/jit(cholesky)/cholesky | solution.py:89
  81.7 0.2 constant_dynamic-update-slice_fusion
  81.9 0.3 convolution_subtract_fusion.2
  82.2 11.7 %cholesky.140 = f32[128,128]{1,0:T(8,128)S(1)} custom-call(f32[128,128]{1,0:T(8,128)S(1)} %convolution_subtract_fusion.2), custom_call_target="Cholesky" | custom-call | tf_op jit(solution)/shard_map/jit(cholesky)/cholesky | solution.py:89
  93.9 0.7 compare_reduce_fusion
  94.7 0.6 compare_reduce_fusion.1
  96.7 0.1 triangular_solve.97
  96.7 4.1 %while.1 = (s32[]{:T(128)}, f32[256,256]{1,0:T(8,128)S(1)}, s32[2,2]{1,0:T(2,128)S(1)}, f32[2,128,128]{2,1,0:T(8,128)S(1)}, s32[]{:T(128)}) while((s32[]{:T(128)}, f32[256,256]{1,0:T(8,128)S(1)}, s32[2,2]{1,0:T(2,128)S(1)}, f32[2,128,128]{2,1,0:T(8,128)S(1)}, s32[]{:T(128)}) %tuple.38), condition=%wide.while_cond, body=%wide.while_body.sunk | while | flops 2 | bytes 131181 | solution.py:90
  96.7 0.6 fusion.61
  97.3 1.4 %bitcast_dynamic-update-slice_fusion.2 = f32[2,128,128]{2,1,0:T(8,128)S(1)} fusion(f32[2,128,128]{2,1,0:T(8,128)S(1)} %get-tuple-element.87, s32[]{:T(128)} %get-tuple-element.84, f32[256,256]{1,0:T(8,128)S(1)} %get-tuple-element.90, s32[]{:T(128)} %bitcast.66, s32[]{:T(128)} %bitcast.67), kind=kLoop, calls=%fused_computation.1.clone.1 | loop fusion | bytes 131084 | tf_op jit(solution)/shard_map/triangular_solve
  98.8 0.6 fusion.61
  99.4 1.4 %bitcast_dynamic-update-slice_fusion.2 = f32[2,128,128]{2,1,0:T(8,128)S(1)} fusion(f32[2,128,128]{2,1,0:T(8,128)S(1)} %get-tuple-element.87, s32[]{:T(128)} %get-tuple-element.84, f32[256,256]{1,0:T(8,128)S(1)} %get-tuple-element.90, s32[]{:T(128)} %bitcast.66, s32[]{:T(128)} %bitcast.67), kind=kLoop, calls=%fused_computation.1.clone.1 | loop fusion | bytes 131084 | tf_op jit(solution)/shard_map/triangular_solve
  100.8 19.7 %custom-call.24 = f32[2,128,128]{1,2,0:T(8,128)S(1)} custom-call(f32[2,128,128]{2,1,0:T(8,128)S(1)} %get-tuple-element.9), custom_call_target="InvertDiagBlocksLowerTriangular" | custom-call | tf_op jit(solution)/shard_map/triangular_solve | solution.py:90
  120.5 0.4 fusion.3
  120.9 0.6 convolution_subtract_fusion.1
  121.5 0.4 fusion.10
  122.0 1.0 copy.24
  123.0 0.8 copy.25
  (28 shorter events, 0.5 us)
Async XLA Ops:
  0.6 13.3 %copy-start = (f32[64]{0:T(128)S(1)}, f32[64]{0:T(128)}, u32[]{:S(2)}) copy-start(f32[64]{0:T(128)} %param.5) | copy-start | bytes 772
  3.2 4.4 %copy-start.1 = (f32[256,256]{1,0:T(8,128)S(1)}, f32[256,256]{1,0:T(8,128)}, u32[]{:S(2)}) copy-start(f32[256,256]{1,0:T(8,128)} %param.7) | copy-start | bytes 786436
  3.2 25.1 %all-to-all-start = ((f32[256,2,512]{0,2,1:T(8,128)}), f32[256,2,512]{0,2,1:T(8,128)S(1)}, u32[]{:S(2)}, u32[]{:S(2)}) async-start(f32[256,2,512]{0,2,1:T(8,128)} %bitcast), calls=%async_computation | async-start | bytes 2097152 | tf_op jit(solution)/shard_map/all_to_all | solution.py:73
  7.6 20.0 %collective-permute-start = (f32[256,256]{1,0:T(8,128)S(1)}, f32[256,256]{1,0:T(8,128)S(1)}, u32[]{:S(2)}, u32[]{:S(2)}) collective-permute-start(f32[256,256]{1,0:T(8,128)S(1)} %copy-done.1), channel_id=1, source_target_pairs={{0,16},{1,17},{2,18},{3,19},{4,20},{5,21},{6,22},{7,23},{8,24},{9,... | collective-permute-start | bytes 786440 | tf_op jit(solution)/shard_map/ppermute | solution.py:33
  13.2 0.7 copy-start.2
  33.7 1.4 %collective-permute-start.1 = (f32[128,256]{0,1:T(8,128)S(1)}, f32[128,256]{0,1:T(8,128)S(1)}, u32[]{:S(2)}, u32[]{:S(2)}) collective-permute-start(f32[128,256]{0,1:T(8,128)S(1)} %constant_dynamic-slice_fusion.1), channel_id=1, source_target_pairs={{0,1},{1,0},{2,3},{3,2},{4,5},{5,4},{6,7},{7,6},{8,9},{9,8},{10,11... | collective-permute-start | bytes 393224 | tf_op jit(solution)/shard_map/ppermute | solution.py:33
  35.1 5.6 %collective-permute-start.2 = (f32[128,256]{0,1:T(8,128)S(1)}, f32[128,256]{0,1:T(8,128)S(1)}, u32[]{:S(2)}, u32[]{:S(2)}) collective-permute-start(f32[128,256]{0,1:T(8,128)S(1)} %dynamic-slice_add_fusion), channel_id=1, source_target_pairs={{0,2},{1,3},{2,0},{3,1},{4,6},{5,7},{6,4},{7,5},{8,10},{9,11},{10,... | collective-permute-start | bytes 393224 | tf_op jit(solution)/shard_map/ppermute | solution.py:33
  40.7 5.0 %collective-permute-start.3 = (f32[128,256]{0,1:T(8,128)S(1)}, f32[128,256]{0,1:T(8,128)S(1)}, u32[]{:S(2)}, u32[]{:S(2)}) collective-permute-start(f32[128,256]{0,1:T(8,128)S(1)} %add.80), channel_id=1, source_target_pairs={{0,4},{1,5},{2,6},{3,7},{4,0},{5,1},{6,2},{7,3},{8,12},{9,13},{10,... | collective-permute-start | bytes 393224 | tf_op jit(solution)/shard_map/ppermute | solution.py:33
  45.8 7.5 %collective-permute-start.4 = (f32[128,256]{0,1:T(8,128)S(1)}, f32[128,256]{0,1:T(8,128)S(1)}, u32[]{:S(2)}, u32[]{:S(2)}) collective-permute-start(f32[128,256]{0,1:T(8,128)S(1)} %add.81), channel_id=1, source_target_pairs={{0,8},{1,9},{2,10},{3,11},{4,12},{5,13},{6,14},{7,15},{8,0},{9,1},... | collective-permute-start | bytes 393224 | tf_op jit(solution)/shard_map/ppermute | solution.py:33
  53.3 5.0 %collective-permute-start.5 = (f32[128,256]{0,1:T(8,128)S(1)}, f32[128,256]{0,1:T(8,128)S(1)}, u32[]{:S(2)}, u32[]{:S(2)}) collective-permute-start(f32[128,256]{0,1:T(8,128)S(1)} %add.82), channel_id=1, source_target_pairs={{0,16},{1,17},{2,18},{3,19},{4,20},{5,21},{6,22},{7,23},{8,24},{9,... | collective-permute-start | bytes 393224 | tf_op jit(solution)/shard_map/ppermute | solution.py:33
  58.3 1.4 %collective-permute-start.6 = (f32[128,256]{0,1:T(8,128)S(1)}, f32[128,256]{0,1:T(8,128)S(1)}, u32[]{:S(2)}, u32[]{:S(2)}) collective-permute-start(f32[128,256]{0,1:T(8,128)S(1)} %add.83), channel_id=1, source_target_pairs={{0,1},{1,0},{2,3},{3,2},{4,5},{5,4},{6,7},{7,6},{8,9},{9,8},{10,11... | collective-permute-start | bytes 393224 | tf_op jit(solution)/shard_map/ppermute | solution.py:33
where the time goes:
time: 124 us
  other arithmetic  59.6 us (48%)
  waiting for transfers between devices  30.4 us (25%)
  starting transfers between devices  14.2 us (11%)
  local copies, waits for them, and re-layouts  9.85 us (8%)
  matrix products  7.48 us (6%)
  between operations  2.3 us (2%)
    another operation x7, other arithmetic, on_device(): lower = jnp.linalg.cholesky(cross)  34.8 us
    ppermute x7, waiting for transfers between devices, swap(): return lax.ppermute(value, AXES, [(i, i ^ bit) for i in range(total)])  30.4 us
    another operation x3, other arithmetic, on_device(): lax.linalg.triangular_solve(lower, sketch, left_side=False, lower=True, t...  19.7 us
    ppermute x7, starting transfers between devices, swap(): return lax.ppermute(value, AXES, [(i, i ^ bit) for i in range(total)])  9.77 us
    all_to_all x1, starting transfers between devices, on_device(): lax.all_to_all(precip, 'tm', split_axis=1, concat_axis=0, tiled=True)  4.39 us
    unnamed x9, local copies, waits for them, and re-layouts  4.38 us
    another operation x6, local copies, waits for them, and re-layouts  4.02 us
  transfers between devices with their start and end apart: 8, of which 7 were waited for; matrix products, arithmetic and copies ran while one was open for 5% of the time, Pallas kernels for 0%

commit v1 on v0

--- a/solution.py
+++ b/solution.py
@@ -70,7 +70,10 @@
         bin_index[:, None] == jnp.arange(thresholds.shape[0], dtype=jnp.int32)[None, :]
     ).astype(jnp.float32)
     level_local = jnp.dot(one_hot, thresholds, precision=highest)
-    series = lax.all_to_all(precip, "tm", split_axis=1, concat_axis=0, tiled=True)
+    series = jnp.concatenate(
+        lax.all_to_all(jnp.stack(jnp.split(precip, lax.axis_size("tm"), axis=1)), "tm", 0, 0),
+        axis=0,
+    )
     projections = jnp.dot(full_table, series, precision=highest)
     coefficients = normal_solve(normal_low, projections)
     anomaly = series - lax.dot_general(

time: 124 us -> 123 us (level)
  local copies, waits for them, and re-layouts: 9.85 us -> 8.15 us
    unnamed x9 -> x8, local copies, waits for them, and re-layouts: 4.38 us -> 1.85 us
    another operation x6 -> x7, local copies, waits for them, and re-layouts: 4.02 us -> 5.19 us
where the time goes in v1:
time: 123 us
  other arithmetic  60.6 us (49%)
  waiting for transfers between devices  30.4 us (25%)
  starting transfers between devices  14.2 us (12%)
  local copies, waits for them, and re-layouts  8.15 us (7%)
  matrix products  7.48 us (6%)
  between operations  2.24 us (2%)
    another operation x7, other arithmetic, on_device(): lower = jnp.linalg.cholesky(cross)  34.8 us
    ppermute x7, waiting for transfers between devices, swap(): return lax.ppermute(value, AXES, [(i, i ^ bit) for i in range(total)])  30.4 us
    another operation x3, other arithmetic, on_device(): lax.linalg.triangular_solve(lower, sketch, left_side=False, lower=True, t...  19.7 us
    ppermute x7, starting transfers between devices, swap(): return lax.ppermute(value, AXES, [(i, i ^ bit) for i in range(total)])  9.77 us
    all_to_all x1, starting transfers between devices, on_device(): lax.all_to_all(jnp.stack(jnp.split(precip, lax.axis_size('tm'), axis=1)),...  4.39 us
    another operation x6, local copies, waits for them, and re-layouts  3.91 us
  transfers between devices with their start and end apart: 8, of which 7 were waited for; matrix products, arithmetic and copies ran while one was open for 5% of the time, Pallas kernels for 0%

profile of v1, /device:TPU:0, one launch (start us, length us, event | category | flops | bytes accessed | tf_op | source)
XLA Modules:
  0.0 123.0 jit_solution(13583939784859081679)
XLA Ops:
  0.6 0.0 copy-start
  0.6 1.3 %slice_bitcast_fusion.1 = (f32[1,256,512]{2,1,0:T(8,128)S(1)}, f32[1,256,512]{2,1,0:T(8,128)S(1)}) fusion(f32[256,1024]{1,0:T(8,128)} %param.4), kind=kLoop, calls=%fused_computation.13 | loop fusion | bytes 2097152 | tf_op jit(solution)/shard_map/stack | solution.py:74
  1.9 1.0 pad_maximum_fusion
  3.0 4.4 %all-to-all-start = ((f32[2,256,512]{2,1,0:T(8,128)}), f32[2,256,512]{2,1,0:T(8,128)S(1)}, u32[]{:S(2)}, u32[]{:S(2)}) async-start(f32[2,256,512]{2,1,0:T(8,128)} %pad_maximum_fusion), calls=%async_computation | async-start | bytes 2097152 | tf_op jit(solution)/shard_map/all_to_all | solution.py:74
  7.4 2.4 %collective-permute-start = (f32[256,256]{1,0:T(8,128)S(1)}, f32[256,256]{1,0:T(8,128)S(1)}, u32[]{:S(2)}, u32[]{:S(2)}) collective-permute-start(f32[256,256]{1,0:T(8,128)S(1)} %copy-done.1), channel_id=1, source_target_pairs={{0,16},{1,17},{2,18},{3,19},{4,20},{5,21},{6,22},{7,23},{8,24},{9,... | collective-permute-start | bytes 786440 | tf_op jit(solution)/shard_map/ppermute | solution.py:33
  9.7 0.1 fusion.21
  9.8 0.1 fusion.23
  9.9 0.1 fusion.25
  10.0 0.1 fusion.27
  10.1 0.1 fusion.29
  10.1 0.1 fusion.31
  10.2 0.1 fusion.33
  10.3 0.1 fusion.35
  10.4 0.1 stack.17
  10.5 0.2 fusion.40
  10.7 0.1 copy.6
  10.8 1.5 %cholesky.60 = f32[17,17]{1,0:T(8,128)S(1)} custom-call(f32[17,17]{1,0:T(8,128)S(1)} %fusion.20), custom_call_target="Cholesky" | custom-call | tf_op jit(solution)/shard_map/jit(cholesky)/cholesky | solution.py:68
  12.4 0.6 compare_reduce_fusion.2
  13.0 0.7 fusion.15
  13.7 0.0 copy-done.2
  13.7 0.4 fusion.2
  14.2 1.3 %custom-call.22 = f32[1,17,17]{1,2,0:T(8,128)S(1)} custom-call(f32[1,17,17]{2,1,0:T(8,128)S(1)} %fusion.15), custom_call_target="InvertDiagBlocksLowerTriangular" | custom-call | tf_op jit(solution)/shard_map/triangular_solve | solution.py:23
  15.5 0.1 dynamic_slice.9
  15.6 11.8 %collective-permute-done = f32[256,256]{1,0:T(8,128)S(1)} collective-permute-done((f32[256,256]{1,0:T(8,128)S(1)}, f32[256,256]{1,0:T(8,128)S(1)}, u32[]{:S(2)}, u32[]{:S(2)}) %collective-permute-start) | collective-permute-done | bytes 262176 | tf_op jit(solution)/shard_map/ppermute | solution.py:33
  27.4 0.6 gather_fusion
  28.0 0.0 all-to-all-done
  28.0 0.6 fusion.41
  28.7 0.2 fusion.18
  28.9 0.2 fusion.16
  29.1 1.1 fusion.1
  30.2 1.8 %fusion.42 = f32[512,256]{1,0:T(8,128)S(1)} fusion(f32[512,512]{1,0:T(8,128)S(1)} %fusion.1, f32[512,256]{1,0:T(8,128)S(1)} %bitcast.72), kind=kOutput, calls=%fused_computation.88 | convolution fusion | flops 805306368 | bytes 2097152 | tf_op jit(solution)/shard_map/dot_general | solution.py:84
  32.0 1.0 fusion.43
  33.1 0.1 collective-permute-start.1
  33.2 1.3 %collective-permute-done.1 = f32[128,256]{0,1:T(8,128)S(1)} collective-permute-done((f32[128,256]{0,1:T(8,128)S(1)}, f32[128,256]{0,1:T(8,128)S(1)}, u32[]{:S(2)}, u32[]{:S(2)}) %collective-permute-start.1) | collective-permute-done | bytes 131104 | tf_op jit(solution)/shard_map/ppermute | solution.py:33
  34.5 1.8 %collective-permute-start.2 = (f32[128,256]{0,1:T(8,128)S(1)}, f32[128,256]{0,1:T(8,128)S(1)}, u32[]{:S(2)}, u32[]{:S(2)}) collective-permute-start(f32[128,256]{0,1:T(8,128)S(1)} %dynamic-slice_add_fusion), channel_id=1, source_target_pairs={{0,2},{1,3},{2,0},{3,1},{4,6},{5,7},{6,4},{7,5},{8,10},{9,11},{10,... | collective-permute-start | bytes 393224 | tf_op jit(solution)/shard_map/ppermute | solution.py:33
  36.3 3.8 %collective-permute-done.2 = f32[128,256]{0,1:T(8,128)S(1)} collective-permute-done((f32[128,256]{0,1:T(8,128)S(1)}, f32[128,256]{0,1:T(8,128)S(1)}, u32[]{:S(2)}, u32[]{:S(2)}) %collective-permute-start.2) | collective-permute-done | bytes 131104 | tf_op jit(solution)/shard_map/ppermute | solution.py:33
  40.2 1.9 %collective-permute-start.3 = (f32[128,256]{0,1:T(8,128)S(1)}, f32[128,256]{0,1:T(8,128)S(1)}, u32[]{:S(2)}, u32[]{:S(2)}) collective-permute-start(f32[128,256]{0,1:T(8,128)S(1)} %add.80), channel_id=1, source_target_pairs={{0,4},{1,5},{2,6},{3,7},{4,0},{5,1},{6,2},{7,3},{8,12},{9,13},{10,... | collective-permute-start | bytes 393224 | tf_op jit(solution)/shard_map/ppermute | solution.py:33
  42.0 3.2 %collective-permute-done.3 = f32[128,256]{0,1:T(8,128)S(1)} collective-permute-done((f32[128,256]{0,1:T(8,128)S(1)}, f32[128,256]{0,1:T(8,128)S(1)}, u32[]{:S(2)}, u32[]{:S(2)}) %collective-permute-start.3) | collective-permute-done | bytes 131104 | tf_op jit(solution)/shard_map/ppermute | solution.py:33
  45.2 2.9 %collective-permute-start.4 = (f32[128,256]{0,1:T(8,128)S(1)}, f32[128,256]{0,1:T(8,128)S(1)}, u32[]{:S(2)}, u32[]{:S(2)}) collective-permute-start(f32[128,256]{0,1:T(8,128)S(1)} %add.81), channel_id=1, source_target_pairs={{0,8},{1,9},{2,10},{3,11},{4,12},{5,13},{6,14},{7,15},{8,0},{9,1},... | collective-permute-start | bytes 393224 | tf_op jit(solution)/shard_map/ppermute | solution.py:33
  48.1 4.6 %collective-permute-done.4 = f32[128,256]{0,1:T(8,128)S(1)} collective-permute-done((f32[128,256]{0,1:T(8,128)S(1)}, f32[128,256]{0,1:T(8,128)S(1)}, u32[]{:S(2)}, u32[]{:S(2)}) %collective-permute-start.4) | collective-permute-done | bytes 131104 | tf_op jit(solution)/shard_map/ppermute | solution.py:33
  52.7 0.7 collective-permute-start.5
  53.5 4.3 %collective-permute-done.5 = f32[128,256]{0,1:T(8,128)S(1)} collective-permute-done((f32[128,256]{0,1:T(8,128)S(1)}, f32[128,256]{0,1:T(8,128)S(1)}, u32[]{:S(2)}, u32[]{:S(2)}) %collective-permute-start.5) | collective-permute-done | bytes 131104 | tf_op jit(solution)/shard_map/ppermute | solution.py:33
  57.8 0.1 collective-permute-start.6
  57.9 1.3 %collective-permute-done.6 = f32[128,256]{0,1:T(8,128)S(1)} collective-permute-done((f32[128,256]{0,1:T(8,128)S(1)}, f32[128,256]{0,1:T(8,128)S(1)}, u32[]{:S(2)}, u32[]{:S(2)}) %collective-permute-start.6) | collective-permute-done | bytes 131104 | tf_op jit(solution)/shard_map/ppermute | solution.py:33
  59.2 0.1 copy.9
  59.4 11.7 %cholesky.123 = f32[128,128]{1,0:T(8,128)S(1)} custom-call(f32[128,128]{1,0:T(8,128)S(1)} %cholesky.153), custom_call_target="Cholesky" | custom-call | tf_op jit(solution)/shard_map/jit(cholesky)/cholesky | solution.py:92
  71.2 10.0 %custom-call.23 = f32[1,128,128]{1,2,0:T(8,128)S(1)} custom-call(f32[1,128,128]{2,1,0:T(8,128)S(1)} %get-tuple-element.29), custom_call_target="InvertDiagBlocksLowerTriangular" | custom-call | tf_op jit(solution)/shard_map/jit(cholesky)/cholesky | solution.py:92
  81.2 0.2 constant_dynamic-update-slice_fusion
  81.4 0.3 convolution_subtract_fusion.2
  81.6 11.7 %cholesky.140 = f32[128,128]{1,0:T(8,128)S(1)} custom-call(f32[128,128]{1,0:T(8,128)S(1)} %convolution_subtract_fusion.2), custom_call_target="Cholesky" | custom-call | tf_op jit(solution)/shard_map/jit(cholesky)/cholesky | solution.py:92
  93.4 0.7 compare_reduce_fusion
  94.1 0.6 compare_reduce_fusion.1
  96.0 0.1 triangular_solve.97
  96.1 3.9 %while.1 = (s32[]{:T(128)}, f32[256,256]{1,0:T(8,128)S(1)}, s32[2,2]{1,0:T(2,128)S(1)}, f32[2,128,128]{2,1,0:T(8,128)S(1)}, s32[]{:T(128)}) while((s32[]{:T(128)}, f32[256,256]{1,0:T(8,128)S(1)}, s32[2,2]{1,0:T(2,128)S(1)}, f32[2,128,128]{2,1,0:T(8,128)S(1)}, s32[]{:T(128)}) %tuple.37), condition=%wide.while_cond, body=%wide.while_body.sunk | while | flops 2 | bytes 131181 | solution.py:93
  96.1 0.6 fusion.61
  96.7 1.4 %bitcast_dynamic-update-slice_fusion.2 = f32[2,128,128]{2,1,0:T(8,128)S(1)} fusion(f32[2,128,128]{2,1,0:T(8,128)S(1)} %get-tuple-element.85, s32[]{:T(128)} %get-tuple-element.82, f32[256,256]{1,0:T(8,128)S(1)} %get-tuple-element.88, s32[]{:T(128)} %bitcast.68, s32[]{:T(128)} %bitcast.69), kind=kLoop, calls=%fused_computation.1.clone.1 | loop fusion | bytes 131084 | tf_op jit(solution)/shard_map/triangular_solve
  98.1 0.6 fusion.61
  98.7 1.4 %bitcast_dynamic-update-slice_fusion.2 = f32[2,128,128]{2,1,0:T(8,128)S(1)} fusion(f32[2,128,128]{2,1,0:T(8,128)S(1)} %get-tuple-element.85, s32[]{:T(128)} %get-tuple-element.82, f32[256,256]{1,0:T(8,128)S(1)} %get-tuple-element.88, s32[]{:T(128)} %bitcast.68, s32[]{:T(128)} %bitcast.69), kind=kLoop, calls=%fused_computation.1.clone.1 | loop fusion | bytes 131084 | tf_op jit(solution)/shard_map/triangular_solve
  100.1 19.7 %custom-call.24 = f32[2,128,128]{1,2,0:T(8,128)S(1)} custom-call(f32[2,128,128]{2,1,0:T(8,128)S(1)} %get-tuple-element.9), custom_call_target="InvertDiagBlocksLowerTriangular" | custom-call | tf_op jit(solution)/shard_map/triangular_solve | solution.py:93
  119.7 0.4 fusion.3
  120.2 0.6 convolution_subtract_fusion.1
  120.7 0.4 fusion.10
  121.2 1.0 copy.10
  122.2 0.8 copy.11
  (28 shorter events, 0.5 us)
Async XLA Ops:
  0.6 13.1 %copy-start = (f32[64]{0:T(128)S(1)}, f32[64]{0:T(128)}, u32[]{:S(2)}) copy-start(f32[64]{0:T(128)} %param.5) | copy-start | bytes 772
  3.0 4.4 %copy-start.1 = (f32[256,256]{1,0:T(8,128)S(1)}, f32[256,256]{1,0:T(8,128)}, u32[]{:S(2)}) copy-start(f32[256,256]{1,0:T(8,128)} %param.7) | copy-start | bytes 786436
  3.0 25.1 %all-to-all-start = ((f32[2,256,512]{2,1,0:T(8,128)}), f32[2,256,512]{2,1,0:T(8,128)S(1)}, u32[]{:S(2)}, u32[]{:S(2)}) async-start(f32[2,256,512]{2,1,0:T(8,128)} %pad_maximum_fusion), calls=%async_computation | async-start | bytes 2097152 | tf_op jit(solution)/shard_map/all_to_all | solution.py:74
  7.4 20.0 %collective-permute-start = (f32[256,256]{1,0:T(8,128)S(1)}, f32[256,256]{1,0:T(8,128)S(1)}, u32[]{:S(2)}, u32[]{:S(2)}) collective-permute-start(f32[256,256]{1,0:T(8,128)S(1)} %copy-done.1), channel_id=1, source_target_pairs={{0,16},{1,17},{2,18},{3,19},{4,20},{5,21},{6,22},{7,23},{8,24},{9,... | collective-permute-start | bytes 786440 | tf_op jit(solution)/shard_map/ppermute | solution.py:33
  13.0 0.7 copy-start.2
  33.1 1.4 %collective-permute-start.1 = (f32[128,256]{0,1:T(8,128)S(1)}, f32[128,256]{0,1:T(8,128)S(1)}, u32[]{:S(2)}, u32[]{:S(2)}) collective-permute-start(f32[128,256]{0,1:T(8,128)S(1)} %constant_dynamic-slice_fusion.1), channel_id=1, source_target_pairs={{0,1},{1,0},{2,3},{3,2},{4,5},{5,4},{6,7},{7,6},{8,9},{9,8},{10,11... | collective-permute-start | bytes 393224 | tf_op jit(solution)/shard_map/ppermute | solution.py:33
  34.5 5.6 %collective-permute-start.2 = (f32[128,256]{0,1:T(8,128)S(1)}, f32[128,256]{0,1:T(8,128)S(1)}, u32[]{:S(2)}, u32[]{:S(2)}) collective-permute-start(f32[128,256]{0,1:T(8,128)S(1)} %dynamic-slice_add_fusion), channel_id=1, source_target_pairs={{0,2},{1,3},{2,0},{3,1},{4,6},{5,7},{6,4},{7,5},{8,10},{9,11},{10,... | collective-permute-start | bytes 393224 | tf_op jit(solution)/shard_map/ppermute | solution.py:33
  40.2 5.0 %collective-permute-start.3 = (f32[128,256]{0,1:T(8,128)S(1)}, f32[128,256]{0,1:T(8,128)S(1)}, u32[]{:S(2)}, u32[]{:S(2)}) collective-permute-start(f32[128,256]{0,1:T(8,128)S(1)} %add.80), channel_id=1, source_target_pairs={{0,4},{1,5},{2,6},{3,7},{4,0},{5,1},{6,2},{7,3},{8,12},{9,13},{10,... | collective-permute-start | bytes 393224 | tf_op jit(solution)/shard_map/ppermute | solution.py:33
  45.2 7.5 %collective-permute-start.4 = (f32[128,256]{0,1:T(8,128)S(1)}, f32[128,256]{0,1:T(8,128)S(1)}, u32[]{:S(2)}, u32[]{:S(2)}) collective-permute-start(f32[128,256]{0,1:T(8,128)S(1)} %add.81), channel_id=1, source_target_pairs={{0,8},{1,9},{2,10},{3,11},{4,12},{5,13},{6,14},{7,15},{8,0},{9,1},... | collective-permute-start | bytes 393224 | tf_op jit(solution)/shard_map/ppermute | solution.py:33
  52.7 5.0 %collective-permute-start.5 = (f32[128,256]{0,1:T(8,128)S(1)}, f32[128,256]{0,1:T(8,128)S(1)}, u32[]{:S(2)}, u32[]{:S(2)}) collective-permute-start(f32[128,256]{0,1:T(8,128)S(1)} %add.82), channel_id=1, source_target_pairs={{0,16},{1,17},{2,18},{3,19},{4,20},{5,21},{6,22},{7,23},{8,24},{9,... | collective-permute-start | bytes 393224 | tf_op jit(solution)/shard_map/ppermute | solution.py:33
  57.8 1.4 %collective-permute-start.6 = (f32[128,256]{0,1:T(8,128)S(1)}, f32[128,256]{0,1:T(8,128)S(1)}, u32[]{:S(2)}, u32[]{:S(2)}) collective-permute-start(f32[128,256]{0,1:T(8,128)S(1)} %add.83), channel_id=1, source_target_pairs={{0,1},{1,0},{2,3},{3,2},{4,5},{5,4},{6,7},{7,6},{8,9},{9,8},{10,11... | collective-permute-start | bytes 393224 | tf_op jit(solution)/shard_map/ppermute | solution.py:33
